TPU v7x, 128 devices: a whole 4x4x4 slice. The times are simulated.
128 devices in a mesh: tm: 32 (over y, z, core), series: 4 (over x).
Axes of the slice: x: 4, y: 4, z: 4, core: 2. Of those that a mesh axis runs over, the one named last changes fastest.
Arguments:
- signal: float32 [64, 1048576], P('series', 'tm')
- valid_start: int32 [64], replicated, may hold values from 0 to 262143
- valid_end: int32 [64], replicated, may hold values from 786433 to 1048576
Outputs:
- smooth: float32 [64, 1048576], P('series', 'tm')
- slope: float32 [64, 1048576], P('series', 'tm')
- covariance: float32 [64, 64], P('series')
Inputs may be any that keep to these rules, and one draw needn't show every extreme that they name: `valid_end`: end of the valid samples of each series.
All inputs are finite; a program needn't handle non-finite values.
Results may differ from a plain program's by a relative error of at most 0.00015.
Values sent between devices are 32-bit elements; how exact they have to be, the bound alone decides.
No kernel may reach another device: no remote copies, remote signals or barrier semaphores. Data moves between devices by JAX's collectives and lax.ppermute only.
A program may use at most 64 MiB of HBM per device.

v0:
```python
import jax
import jax.numpy as jnp
from jax import lax
from jax.sharding import PartitionSpec as P

HALF = 16


def padded(cells, sides, width):
    for axis, dim in sides:
        count = lax.axis_size(axis)
        ends = count - 1
        head = lax.slice_in_dim(cells, 0, width, axis=dim)
        tail = lax.slice_in_dim(cells, cells.shape[dim] - width, cells.shape[dim], axis=dim)
        cells = jnp.concatenate(
            [
                lax.ppermute(tail, axis, [(i, (i + 1) % count) for i in range(ends)]),
                cells,
                lax.ppermute(head, axis, [((i + 1) % count, i) for i in range(ends)]),
            ],
            axis=dim,
        )
    return cells


def split_up(shard, dim, count):
    before, after = (shard.shape[:dim], shard.shape[dim + 1 :])
    return jnp.moveaxis(shard.reshape(*before, count, -1, *after), dim, 0)


def summed_on_arrival(shard, axis, dim):
    count = lax.axis_size(axis)
    tiles = lax.all_to_all(split_up(shard, dim, count), axis, 0, 0, tiled=True)
    return jnp.sum(tiles, axis=0)


def from_everyone(shard, axis):
    copies = jnp.broadcast_to(shard, (lax.axis_size(axis), *shard.shape))
    return lax.all_to_all(copies, axis, split_axis=0, concat_axis=0, tiled=True)


def over_copies(shard, axis):
    return from_everyone(shard, axis).sum(axis=0)


def cross_rows(left, right):
    return lax.dot_general(
        left,
        right,
        (((1,), (1,)), ((), ())),
        precision=lax.Precision.HIGHEST,
        preferred_element_type=jnp.float32,
    )


def held_value(field, spot):
    return jnp.take_along_axis(field, spot, axis=1)


def shards(signal, valid_start, valid_end):
    rows, width = signal.shape
    taps = 2 * HALF + 1
    offsets = jnp.arange(-HALF, HALF + 1).astype(jnp.float32)
    second = jnp.sum(offsets * offsets)
    centre_sq = second / taps
    curved = offsets * offsets - centre_sq
    fourth = jnp.sum(curved * curved)
    extended = padded(signal, (("tm", 1),), 2 * HALF)
    span = width + 2 * HALF
    level = jnp.zeros((rows, span), jnp.float32)
    tilt = jnp.zeros((rows, span), jnp.float32)
    bend = jnp.zeros((rows, span), jnp.float32)
    for m in range(taps):
        window = extended[:, m : m + span]
        level = level + window * (1.0 / taps)
        tilt = tilt + window * (offsets[m] / second)
        bend = bend + window * (curved[m] / fourth)
    begin = lax.axis_index("tm") * width
    group = lax.axis_index("series") * rows
    first = lax.dynamic_slice_in_dim(valid_start, group, rows)[:, None]
    last = lax.dynamic_slice_in_dim(valid_end, group, rows)[:, None]
    moment = begin + jnp.arange(width, dtype=jnp.int32)[None, :]
    low_centre = first + HALF
    high_centre = last - HALF - 1
    centre = jnp.clip(moment, low_centre, high_centre)
    low_spot = jnp.clip(low_centre - begin + HALF, 0, span - 1)
    high_spot = jnp.clip(high_centre - begin + HALF, 0, span - 1)
    below = moment < low_centre
    above = moment > high_centre
    along = (moment - centre).astype(jnp.float32)
    lv = jnp.where(
        below,
        held_value(level, low_spot),
        jnp.where(above, held_value(level, high_spot), level[:, HALF : HALF + width]),
    )
    tl = jnp.where(
        below,
        held_value(tilt, low_spot),
        jnp.where(above, held_value(tilt, high_spot), tilt[:, HALF : HALF + width]),
    )
    bd = jnp.where(
        below,
        held_value(bend, low_spot),
        jnp.where(above, held_value(bend, high_spot), bend[:, HALF : HALF + width]),
    )
    inside = (moment >= first) & (moment < last)
    smooth = jnp.where(inside, lv + tl * along + bd * (along * along - centre_sq), 0.0)
    slope = jnp.where(inside, HALF * (tl + 2.0 * along * bd), 0.0)
    resid = jnp.where(inside, signal - smooth, 0.0)
    mixed = lax.all_to_all(resid, "series", split_axis=1, concat_axis=0, tiled=True)
    gram = summed_on_arrival(cross_rows(mixed, mixed), "series", 0)
    gram = over_copies(gram, "tm")
    correlation = (
        jnp.minimum(last, valid_end[None, :]) - jnp.maximum(first, valid_start[None, :])
    ).astype(jnp.float32)
    return (smooth, slope, gram / correlation)


def solution(mesh):
    in_specs = (P("series", "tm"), P(), P())
    out_specs = (P("series", "tm"), P("series", "tm"), P("series", None))
    return jax.shard_map(shards, mesh=mesh, in_specs=in_specs, out_specs=out_specs, check_vma=False)
```

profile of v0, /device:TPU:1, one launch (start us, length us, event | category | flops | bytes accessed | tf_op | source)
XLA Modules:
  0.0 243.7 jit_solution(17497777037096725441)
XLA Ops:
  0.6 0.8 fusion.16
  1.4 4.9 %collective-permute-start = (f32[16,32]{1,0:T(8,128)S(1)}, f32[16,32]{1,0:T(8,128)S(1)}, u32[]{:S(2)}, u32[]{:S(2)}) collective-permute-start(f32[16,32]{1,0:T(8,128)S(1)} %get-tuple-element.11), channel_id=1, source_target_pairs={{0,4},{4,8},{8,12},{12,16},{16,20},{20,24},{24,28},{28,32},{32,36}... | collective-permute-start | bytes 6152 | tf_op jit(solution)/shard_map/ppermute | solution.py:17
  6.3 1.9 collective-permute-start.1
  8.9 0.7 fusion.17
  9.6 0.7 fusion.18
  10.3 3.1 %constant_dynamic-update-slice_fusion.1 = f32[16,32800]{1,0:T(8,128)} fusion(f32[16,32768]{1,0:T(8,128)} %param.5), kind=kLoop, calls=%fused_computation.29 | loop fusion | bytes 4194304
  14.7 0.7 fusion.19
  15.4 0.7 fusion.20
  101.8 6.4 %dynamic-update-slice.3 = f32[16,32832]{1,0:T(8,128)S(1)} dynamic-update-slice(f32[16,32832]{1,0:T(8,128)S(1)} %dynamic-update-slice.2, f32[16,32768]{1,0:T(8,128)} %param.5, s32[]{} %constant.163, s32[]{} %constant.165) | dynamic-update-slice | bytes 4194308
  108.9 19.9 %multiply_add_fusion.1 = f32[16,32800]{1,0:T(8,128)} fusion(f32[16,32800]{1,0:T(8,128)} %constant_dynamic-update-slice_fusion, f32[16,32832]{1,0:T(8,128)S(1)} %dynamic-update-slice.4, f32[16,32768]{1,0:T(8,128)} %param.5, f32[16,32]{1,0:T(8,128)S(1)} %collective-permute-done, f32[]{:T(128)S(6)} %div.236, f32[]{:T(128)S(6)} %div.235, f32[]{:T(128)S(6)} %div.234, ...), kind=kLoop, calls=%fused_computation.15 | loop fusion | flops 34636800 | bytes 71372928 | tf_op jit(solution)/shard_map/add | solution.py:76
  128.8 1.6 gather_fusion.2
  130.4 1.6 gather_fusion.3
  132.0 19.9 %multiply_add_fusion = f32[16,32800]{1,0:T(8,128)} fusion(f32[16,32800]{1,0:T(8,128)} %constant_dynamic-update-slice_fusion, f32[16,32832]{1,0:T(8,128)S(1)} %dynamic-update-slice.4, f32[16,32768]{1,0:T(8,128)} %param.5, f32[16,32]{1,0:T(8,128)S(1)} %collective-permute-done, f32[]{:T(128)S(6)} %div.270, f32[]{:T(128)S(6)} %div.269, f32[]{:T(128)S(6)} %div.268, ...), kind=kLoop, calls=%fused_computation.14 | loop fusion | flops 34636800 | bytes 71372928 | tf_op jit(solution)/shard_map/add | solution.py:77
  151.9 1.6 gather_fusion.4
  153.5 1.6 gather_fusion.5
  155.1 19.9 %add_multiply_fusion = f32[16,32800]{1,0:T(8,128)} fusion(f32[16,32800]{1,0:T(8,128)} %constant_dynamic-update-slice_fusion, f32[16,32832]{1,0:T(8,128)S(1)} %dynamic-update-slice.4, f32[16,32768]{1,0:T(8,128)} %param.5, f32[16,32]{1,0:T(8,128)S(1)} %collective-permute-done), kind=kLoop, calls=%fused_computation.13 | loop fusion | flops 17843200 | bytes 71372800 | tf_op jit(solution)/shard_map/add | solution.py:75
  175.0 1.6 gather_fusion
  176.6 1.7 gather_fusion.1
  178.2 6.0 %subtract_select_fusion = (f32[16,32768]{1,0:T(8,128)S(1)}, f32[16,32768]{1,0:T(8,128)}, f32[16,32768]{1,0:T(8,128)}) fusion(f32[16,32768]{1,0:T(8,128)} %param.5, s32[32768]{0:T(1024)S(1)} %iota_add_fusion, s32[16]{0:T(128)S(1)} %get-tuple-element.9, s32[16]{0:T(128)S(1)} %get-tuple-element.7, f32[]{:T(128)S(6)} %div.237, f32[16,32800]{1,0:T(8,128)} %multiply_add_fusion, ...), kind=kLoop, calls=%fused_computation.22 | loop fusion | flops 15204352 | bytes 14811780 | tf_op jit(solution)/shard_map/jit(_where)/select_n | solution.py:109
  184.3 29.0 %all_to_all.29 = f32[16,4,8192]{2,0,1:T(8,128)S(1)} all-to-all(f32[16,4,8192]{2,0,1:T(8,128)S(1)} %bitcast.164), channel_id=1, replica_groups=mesh['tm'=32,'series'=4] {'series'}, dimensions={1} | all-to-all | bytes 4194304 | tf_op jit(solution)/shard_map/all_to_all | solution.py:110
  213.4 1.8 fusion.3
  215.3 6.6 %all_to_all.30 = f32[4,1,1024]{2,1,0:T(1,128)S(1)} all-to-all(f32[4,1,1024]{2,1,0:T(1,128)S(1)} %reshape.138), channel_id=1, replica_groups=mesh['tm'=32,'series'=4] {'series'}, dimensions={0} | all-to-all | bytes 32768 | tf_op jit(solution)/shard_map/all_to_all | solution.py:33
  223.4 18.5 %all_to_all.31 = f32[32,1,1024]{2,1,0:T(1,128)S(1)} all-to-all(f32[32,1,1024]{2,1,0:T(1,128)S(1)} %reshape.140), channel_id=1, replica_groups=mesh['tm'=32,'series'=4] {'tm'}, dimensions={0} | all-to-all | bytes 262144 | tf_op jit(solution)/shard_map/all_to_all | solution.py:39
  241.9 1.0 reduce.1
  (35 shorter events, 5.1 us)
Async XLA Ops:
  1.4 100.1 %collective-permute-start = (f32[16,32]{1,0:T(8,128)S(1)}, f32[16,32]{1,0:T(8,128)S(1)}, u32[]{:S(2)}, u32[]{:S(2)}) collective-permute-start(f32[16,32]{1,0:T(8,128)S(1)} %get-tuple-element.11), channel_id=1, source_target_pairs={{0,4},{4,8},{8,12},{12,16},{16,20},{20,24},{24,28},{28,32},{32,36}... | collective-permute-start | bytes 6152 | tf_op jit(solution)/shard_map/ppermute | solution.py:17
  6.3 101.8 %collective-permute-start.1 = (f32[16,32]{1,0:T(8,128)S(1)}, f32[16,32]{1,0:T(8,128)S(1)}, u32[]{:S(2)}, u32[]{:S(2)}) collective-permute-start(f32[16,32]{1,0:T(8,128)S(1)} %get-tuple-element.12), channel_id=1, source_target_pairs={{4,0},{8,4},{12,8},{16,12},{20,16},{24,20},{28,24},{32,28},{36,32}... | collective-permute-start | bytes 6152 | tf_op jit(solution)/shard_map/ppermute | solution.py:19
  10.3 49.0 %copy-start.1 = (s32[64]{0:T(128)S(1)}, s32[64]{0:T(128)}, u32[]{:S(2)}) copy-start(s32[64]{0:T(128)} %param.6) | copy-start | bytes 772
  10.3 49.1 %copy-start = (s32[64]{0:T(128)S(1)}, s32[64]{0:T(128)}, u32[]{:S(2)}) copy-start(s32[64]{0:T(128)} %param.7) | copy-start | bytes 772
where the time goes:
time: 246 us; the launch traced here: 244 us
  between operations  86.5 us (35%)
  other arithmetic  69.5 us (28%)
  blocking collectives  54.1 us (22%)
  local copies, waits for them, and re-layouts  24.9 us (10%)
  starting transfers between devices  6.83 us (3%)
    all_to_all x1, blocking collectives, shards(): lax.all_to_all(resid, 'series', split_axis=1, concat_axis=0, tiled=True)  29 us
    add x1, other arithmetic, shards(): bend = bend + window * (curved[m] / fourth)  19.9 us
    add x1, other arithmetic, shards(): tilt = tilt + window * (offsets[m] / second)  19.9 us
    add x1, other arithmetic, shards(): level = level + window * (1.0 / taps)  19.9 us
    all_to_all x1, blocking collectives, from_everyone(): return lax.all_to_all(copies, axis, split_axis=0, concat_axis=0, tiled=True)  18.5 us
    unnamed x11, local copies, waits for them, and re-layouts  10.2 us
    gather x6, local copies, waits for them, and re-layouts, held_value(): return jnp.take_along_axis(field, spot, axis=1)  9.65 us
    all_to_all x1, blocking collectives, summed_on_arrival(): tiles = lax.all_to_all(split_up(shard, dim, count), axis, 0, 0, tiled=True)  6.56 us
  transfers between devices with their start and end apart: 2, of which 0 were waited for; matrix products, arithmetic and copies ran while one was open for 6% of the time, Pallas kernels for 0%

commit v1 on v0

--- a/solution.py
+++ b/solution.py
@@ -2,6 +2,7 @@
 import jax.numpy as jnp
 from jax import lax
 from jax.sharding import PartitionSpec as P
+from jax.lax import axis_index, axis_size, ppermute
 
 HALF = 16
 
@@ -107,7 +108,18 @@
     smooth = jnp.where(inside, lv + tl * along + bd * (along * along - centre_sq), 0.0)
     slope = jnp.where(inside, HALF * (tl + 2.0 * along * bd), 0.0)
     resid = jnp.where(inside, signal - smooth, 0.0)
-    mixed = lax.all_to_all(resid, "series", split_axis=1, concat_axis=0, tiled=True)
+    y1, o_now = (axis_size("series"), axis_index("series"))
+    answer = resid.shape[1] // y1
+    aux = jnp.roll(resid, -o_now * answer, 1)
+    tray = [lax.slice_in_dim(aux, 0, answer, axis=1)]
+    d = 1
+    while d < y1:
+        prior = lax.slice_in_dim(aux, d * answer, (d + 1) * answer, axis=1)
+        base_arr = ppermute(prior, "series", perm=[(num, (num + d) % y1) for num in range(y1)])
+        tray.append(base_arr)
+        d += 1
+    mat_out = jnp.concatenate(tray[::-1], 0)
+    mixed = jnp.roll(mat_out, (o_now + 1) * tray[0].shape[0], 0)
     gram = summed_on_arrival(cross_rows(mixed, mixed), "series", 0)
     gram = over_copies(gram, "tm")
     correlation = (

time: 246 us -> 247 us (level)
  blocking collectives: 54.1 us -> 23.9 us
  waiting for transfers between devices: 0.01 us -> 25.4 us
  starting transfers between devices: 6.83 us -> 10.5 us
    all_to_all x1 -> x0, blocking collectives: 29 us -> none  [shards(): lax.all_to_all(resid, 'series', split_axis=1, concat_axis=0, tiled=True)]
    ppermute x0 -> x3, waiting for transfers between devices: none -> 25.4 us  [shards(): ppermute(prior, 'series', perm=[(num, (num + d) % y1) for num in range(y1)])]
    ppermute x0 -> x3, starting transfers between devices: none -> 3.71 us  [shards(): ppermute(prior, 'series', perm=[(num, (num + d) % y1) for num in range(y1)])]
    unnamed x11 -> x18, local copies, waits for them, and re-layouts: 10.2 us -> 10.5 us
  transfers between devices with their start and end apart: 2 -> 5, of which waited for: 0 -> 2; matrix products, arithmetic and copies ran while one was open for 6% -> 6% of each run, Pallas kernels for 0% -> 0%
where the time goes in v1:
time: 247 us; the launch traced here: 245 us
  between operations  87 us (35%)
  other arithmetic  70 us (28%)
  local copies, waits for them, and re-layouts  26.2 us (11%)
  waiting for transfers between devices  25.4 us (10%)
  blocking collectives  23.9 us (10%)
  starting transfers between devices  10.5 us (4%)
    ppermute x3, waiting for transfers between devices, shards(): ppermute(prior, 'series', perm=[(num, (num + d) % y1) for num in range(y1)])  25.4 us
    add x1, other arithmetic, shards(): tilt = tilt + window * (offsets[m] / second)  19.9 us
    add x1, other arithmetic, shards(): bend = bend + window * (curved[m] / fourth)  19.9 us
    add x1, other arithmetic, shards(): level = level + window * (1.0 / taps)  19.9 us
    all_to_all x1, blocking collectives, from_everyone(): return lax.all_to_all(copies, axis, split_axis=0, concat_axis=0, tiled=True)  17.3 us
    unnamed x18, local copies, waits for them, and re-layouts  10.5 us
    gather x6, local copies, waits for them, and re-layouts, held_value(): return jnp.take_along_axis(field, spot, axis=1)  9.65 us
    all_to_all x1, blocking collectives, summed_on_arrival(): tiles = lax.all_to_all(split_up(shard, dim, count), axis, 0, 0, tiled=True)  6.56 us
  transfers between devices with their start and end apart: 5, of which 2 were waited for; matrix products, arithmetic and copies ran while one was open for 6% of the time, Pallas kernels for 0%

profile of v1, /device:TPU:1, one launch (start us, length us, event | category | flops | bytes accessed | tf_op | source)
XLA Modules:
  0.0 244.8 jit_solution(14469922633675364502)
XLA Ops:
  0.6 0.8 fusion.19
  1.4 3.3 %collective-permute-start.1 = (f32[16,32]{1,0:T(8,128)S(1)}, f32[16,32]{1,0:T(8,128)S(1)}, u32[]{:S(2)}, u32[]{:S(2)}) collective-permute-start(f32[16,32]{1,0:T(8,128)S(1)} %get-tuple-element.15), channel_id=1, source_target_pairs={{4,0},{8,4},{12,8},{16,12},{20,16},{24,20},{28,24},{32,28},{36,32}... | collective-permute-start | bytes 6152 | tf_op jit(solution)/shard_map/ppermute | solution.py:20
  4.7 3.6 %collective-permute-start = (f32[16,32]{1,0:T(8,128)S(1)}, f32[16,32]{1,0:T(8,128)S(1)}, u32[]{:S(2)}, u32[]{:S(2)}) collective-permute-start(f32[16,32]{1,0:T(8,128)S(1)} %get-tuple-element.14), channel_id=1, source_target_pairs={{0,4},{4,8},{8,12},{12,16},{16,20},{20,24},{24,28},{28,32},{32,36}... | collective-permute-start | bytes 6152 | tf_op jit(solution)/shard_map/ppermute | solution.py:18
  8.9 3.1 %constant_dynamic-update-slice_fusion.1 = f32[16,32800]{1,0:T(8,128)} fusion(f32[16,32768]{1,0:T(8,128)} %param.5), kind=kLoop, calls=%fused_computation.32 | loop fusion | bytes 4194304
  102.2 6.4 %dynamic-update-slice.11 = f32[16,32832]{1,0:T(8,128)S(1)} dynamic-update-slice(f32[16,32832]{1,0:T(8,128)S(1)} %dynamic-update-slice.10, f32[16,32768]{1,0:T(8,128)} %param.5, s32[]{} %constant.203, s32[]{} %constant.205) | dynamic-update-slice | bytes 4194308
  109.3 19.9 %multiply_add_fusion.1 = f32[16,32800]{1,0:T(8,128)} fusion(f32[16,32800]{1,0:T(8,128)} %constant_dynamic-update-slice_fusion, f32[16,32832]{1,0:T(8,128)S(1)} %dynamic-update-slice.12, f32[16,32768]{1,0:T(8,128)} %param.5, f32[16,32]{1,0:T(8,128)S(1)} %collective-permute-done, f32[]{:T(128)S(6)} %div.236, f32[]{:T(128)S(6)} %div.235, f32[]{:T(128)S(6)} %div.234, ...), kind=kLoop, calls=%fused_computation.17 | loop fusion | flops 34636800 | bytes 71372928 | tf_op jit(solution)/shard_map/add | solution.py:77
  129.2 1.6 gather_fusion.3
  130.8 19.9 %multiply_add_fusion = f32[16,32800]{1,0:T(8,128)} fusion(f32[16,32800]{1,0:T(8,128)} %constant_dynamic-update-slice_fusion, f32[16,32832]{1,0:T(8,128)S(1)} %dynamic-update-slice.12, f32[16,32768]{1,0:T(8,128)} %param.5, f32[16,32]{1,0:T(8,128)S(1)} %collective-permute-done, f32[]{:T(128)S(6)} %div.270, f32[]{:T(128)S(6)} %div.269, f32[]{:T(128)S(6)} %div.268, ...), kind=kLoop, calls=%fused_computation.16 | loop fusion | flops 34636800 | bytes 71372928 | tf_op jit(solution)/shard_map/add | solution.py:78
  150.7 1.6 gather_fusion.5
  152.3 1.6 gather_fusion.4
  153.9 1.6 gather_fusion.2
  155.5 19.9 %add_multiply_fusion = f32[16,32800]{1,0:T(8,128)} fusion(f32[16,32800]{1,0:T(8,128)} %constant_dynamic-update-slice_fusion, f32[16,32832]{1,0:T(8,128)S(1)} %dynamic-update-slice.12, f32[16,32768]{1,0:T(8,128)} %param.5, f32[16,32]{1,0:T(8,128)S(1)} %collective-permute-done), kind=kLoop, calls=%fused_computation.15 | loop fusion | flops 17843200 | bytes 71372800 | tf_op jit(solution)/shard_map/add | solution.py:76
  175.4 1.6 gather_fusion.1
  177.0 1.6 gather_fusion
  178.6 6.0 %subtract_select_fusion = (f32[16,32768]{1,0:T(8,128)S(1)}, f32[16,32768]{1,0:T(8,128)}, f32[16,32768]{1,0:T(8,128)}) fusion(f32[16,32768]{1,0:T(8,128)} %param.5, s32[32768]{0:T(1024)S(1)} %iota_add_fusion, s32[16]{0:T(128)S(1)} %get-tuple-element.9, s32[16]{0:T(128)S(1)} %get-tuple-element.7, f32[]{:T(128)S(6)} %div.237, f32[16,32800]{1,0:T(8,128)} %multiply_add_fusion, ...), kind=kLoop, calls=%fused_computation.24 | loop fusion | flops 15204352 | bytes 14811780 | tf_op jit(solution)/shard_map/jit(_where)/select_n | solution.py:110
  185.2 1.1 fusion.18
  186.3 2.6 %collective-permute-start.2 = (f32[16,8192]{1,0:T(8,128)}, f32[16,8192]{1,0:T(8,128)S(1)}, u32[]{:S(2)}, u32[]{:S(2)}) collective-permute-start(f32[16,8192]{1,0:T(8,128)} %get-tuple-element.13), channel_id=1, source_target_pairs={{0,3},{1,0},{2,1},{3,2},{4,7},{5,4},{6,5},{7,6},{8,11},{9,8},{10,9... | collective-permute-start | bytes 1572872 | tf_op jit(solution)/shard_map/ppermute | solution.py:118
  189.2 0.8 collective-permute-start.4
  190.0 21.6 %collective-permute-done.2 = f32[16,8192]{1,0:T(8,128)S(1)} collective-permute-done((f32[16,8192]{1,0:T(8,128)}, f32[16,8192]{1,0:T(8,128)S(1)}, u32[]{:S(2)}, u32[]{:S(2)}) %collective-permute-start.2) | collective-permute-done | bytes 524320 | tf_op jit(solution)/shard_map/ppermute | solution.py:118
  211.7 3.8 %collective-permute-done.4 = f32[16,8192]{1,0:T(8,128)S(1)} collective-permute-done((f32[16,8192]{1,0:T(8,128)S(1)}, f32[16,8192]{1,0:T(8,128)S(1)}, u32[]{:S(2)}, u32[]{:S(2)}) %collective-permute-start.4) | collective-permute-done | bytes 524320 | tf_op jit(solution)/shard_map/ppermute | solution.py:118
  215.7 1.8 fusion.4
  217.6 6.6 %all_to_all.10 = f32[4,1,1024]{2,1,0:T(1,128)S(1)} all-to-all(f32[4,1,1024]{2,1,0:T(1,128)S(1)} %reshape.135), channel_id=1, replica_groups=mesh['tm'=32,'series'=4] {'series'}, dimensions={0} | all-to-all | bytes 32768 | tf_op jit(solution)/shard_map/all_to_all | solution.py:34
  225.7 17.3 %all_to_all.11 = f32[32,1,1024]{2,1,0:T(1,128)S(1)} all-to-all(f32[32,1,1024]{2,1,0:T(1,128)S(1)} %reshape.137), channel_id=1, replica_groups=mesh['tm'=32,'series'=4] {'tm'}, dimensions={0} | all-to-all | bytes 262144 | tf_op jit(solution)/shard_map/all_to_all | solution.py:40
  243.0 1.0 reduce.1
  (49 shorter events, 9.1 us)
Async XLA Ops:
  1.4 107.1 %collective-permute-start.1 = (f32[16,32]{1,0:T(8,128)S(1)}, f32[16,32]{1,0:T(8,128)S(1)}, u32[]{:S(2)}, u32[]{:S(2)}) collective-permute-start(f32[16,32]{1,0:T(8,128)S(1)} %get-tuple-element.15), channel_id=1, source_target_pairs={{4,0},{8,4},{12,8},{16,12},{20,16},{24,20},{28,24},{32,28},{36,32}... | collective-permute-start | bytes 6152 | tf_op jit(solution)/shard_map/ppermute | solution.py:20
  4.7 97.2 %collective-permute-start = (f32[16,32]{1,0:T(8,128)S(1)}, f32[16,32]{1,0:T(8,128)S(1)}, u32[]{:S(2)}, u32[]{:S(2)}) collective-permute-start(f32[16,32]{1,0:T(8,128)S(1)} %get-tuple-element.14), channel_id=1, source_target_pairs={{0,4},{4,8},{8,12},{12,16},{16,20},{20,24},{24,28},{28,32},{32,36}... | collective-permute-start | bytes 6152 | tf_op jit(solution)/shard_map/ppermute | solution.py:18
  8.9 7.3 %copy-start = (s32[64]{0:T(128)S(1)}, s32[64]{0:T(128)}, u32[]{:S(2)}) copy-start(s32[64]{0:T(128)} %param.7) | copy-start | bytes 772
  8.9 7.4 %copy-start.1 = (s32[64]{0:T(128)S(1)}, s32[64]{0:T(128)}, u32[]{:S(2)}) copy-start(s32[64]{0:T(128)} %param.6) | copy-start | bytes 772
  186.3 25.3 %collective-permute-start.2 = (f32[16,8192]{1,0:T(8,128)}, f32[16,8192]{1,0:T(8,128)S(1)}, u32[]{:S(2)}, u32[]{:S(2)}) collective-permute-start(f32[16,8192]{1,0:T(8,128)} %get-tuple-element.13), channel_id=1, source_target_pairs={{0,3},{1,0},{2,1},{3,2},{4,7},{5,4},{6,5},{7,6},{8,11},{9,8},{10,9... | collective-permute-start | bytes 1572872 | tf_op jit(solution)/shard_map/ppermute | solution.py:118
  188.9 22.8 %collective-permute-start.3 = (f32[16,8192]{1,0:T(8,128)}, f32[16,8192]{1,0:T(8,128)S(1)}, u32[]{:S(2)}, u32[]{:S(2)}) collective-permute-start(f32[16,8192]{1,0:T(8,128)} %get-tuple-element.12), channel_id=1, source_target_pairs={{0,2},{1,3},{2,0},{3,1},{4,6},{5,7},{6,4},{7,5},{8,10},{9,11},{10,... | collective-permute-start | bytes 1572872 | tf_op jit(solution)/shard_map/ppermute | solution.py:118
  189.2 26.2 %collective-permute-start.4 = (f32[16,8192]{1,0:T(8,128)S(1)}, f32[16,8192]{1,0:T(8,128)S(1)}, u32[]{:S(2)}, u32[]{:S(2)}) collective-permute-start(f32[16,8192]{1,0:T(8,128)S(1)} %get-tuple-element.11), channel_id=1, source_target_pairs={{0,1},{1,2},{2,3},{3,0},{4,5},{5,6},{6,7},{7,4},{8,9},{9,10},{10,1... | collective-permute-start | bytes 1572872 | tf_op jit(solution)/shard_map/ppermute | solution.py:118
